TPU v7x, 256 devices: a whole 4x4x8 slice. The times are simulated.
256 devices in a mesh: chol: 16 (over x, y), walker: 8 (over z), orb: 2 (over core).
Axes of the slice: x: 4, y: 4, z: 8, core: 2. Of those that a mesh axis runs over, the one named last changes fastest.
Arguments:
- chol_vals: bfloat16 [4096, 4, 64, 128], P('chol', 'orb'), may hold values from -0.05 to 0.05, as said below
- chol_cols: int32 [4096, 4, 2], P('chol', 'orb'), may hold values from 0 to 4, as said below
- greens: bfloat16 [256, 256, 256], P('walker', 'orb'), may hold values from -0.75 to 0.75
- walkers: bfloat16 [256, 256, 128], P('walker', 'orb'), may hold values from -6 to 6
- fields: float32 [4096, 256], P('chol', 'walker'), may hold values from -6 to 6
Outputs:
- new_walkers: bfloat16 [256, 256, 128], P('walker', 'orb')
- energy: float32 [256], P('walker')
Inputs may be any that keep to these rules, and one draw needn't show every extreme that they name: `chol_cols`: for every vector g and block row r, slot 0 holds r; the other slots hold distinct block columns different from r, or 4 for an empty slot. `chol_vals`: values of the stored blocks; entries in empty slots are not used.
All inputs are finite; a program needn't handle non-finite values.
Results may differ from a plain program's by a relative error of at most 0.0055.
Values may be sent and summed in bfloat16 or wider, within the bound.
A program may use at most 128 MiB of HBM per device.

v0:
```python
import jax
import jax.numpy as jnp
from jax import lax
from jax.sharding import PartitionSpec as P

NORB = 256
BLOCK = 64
SLOTS = 2
TAYLOR = 4
ROWBLK = 4


def dense_rows(values, columns):
    vectors = values.shape[0]
    row_blocks = values.shape[1]
    pieces = values.reshape(vectors, row_blocks, BLOCK, SLOTS, BLOCK)
    onehot = (columns[..., None] == jnp.arange(ROWBLK, dtype=jnp.int32)).astype(jnp.bfloat16)
    placed = jnp.einsum("grsc,grisj->gricj", onehot, pieces, preferred_element_type=jnp.float32)
    return placed.astype(jnp.bfloat16).reshape(vectors, row_blocks * BLOCK * NORB)


def per_device(chol_vals, chol_cols, greens, walkers, fields):
    vectors = chol_vals.shape[0]
    walk_count = greens.shape[0]
    half_rows = greens.shape[1]
    step_factor = 72.0 / float(vectors * lax.axis_size("chol") * BLOCK) ** 0.5
    matrix = dense_rows(chol_vals, chol_cols)
    green_flat = greens.reshape(walk_count, half_rows * NORB)
    partial_bias = lax.dot_general(
        matrix, green_flat, (((1,), (1,)), ((), ())), preferred_element_type=jnp.float32
    )
    force_bias = lax.psum(partial_bias.astype(jnp.bfloat16), "orb").astype(jnp.float32)
    energy = lax.psum(0.5 * jnp.sum(force_bias * force_bias, axis=0), "chol")
    shifted = (fields - force_bias).astype(jnp.bfloat16)
    own_count = walk_count // lax.axis_size("chol")
    summed = lax.dot_general(
        shifted, matrix, (((0,), (0,)), ((), ())), preferred_element_type=jnp.float32
    )
    summed_field = lax.psum_scatter(
        summed.reshape(own_count * lax.axis_size("chol"), half_rows, NORB),
        "chol",
        scatter_dimension=0,
        tiled=True,
    )
    potential = (step_factor * summed_field).astype(jnp.bfloat16)
    first_walker = lax.axis_index("chol") * own_count
    start_rows = lax.dynamic_slice_in_dim(walkers, first_walker, own_count, 0)
    series_term = start_rows
    series_sum = jnp.zeros(start_rows.shape, jnp.float32)
    for degree in range(1, TAYLOR + 1):
        full_rows = lax.all_gather(series_term, "orb", axis=1, tiled=True)
        product = jnp.einsum(
            "wij,wja->wia", potential, full_rows, preferred_element_type=jnp.float32
        )
        series_term = (product / degree).astype(jnp.bfloat16)
        series_sum = series_sum + series_term.astype(jnp.float32)
    moved = (start_rows.astype(jnp.float32) + series_sum).astype(jnp.bfloat16)
    new_walkers = lax.all_gather(moved, "chol", axis=0, tiled=True)
    return (new_walkers, energy)


def solution(mesh):
    in_specs = (
        P("chol", "orb", None, None),
        P("chol", "orb", None),
        P("walker", "orb", None),
        P("walker", "orb", None),
        P("chol", "walker"),
    )
    out_specs = (P("walker", "orb", None), P("walker"))
    return jax.shard_map(
        per_device, mesh=mesh, in_specs=in_specs, out_specs=out_specs, check_vma=False
    )
```

profile of v0, /device:TPU:160, one launch (start us, length us, event | category | flops | bytes accessed | tf_op | source)
XLA Modules:
  0.0 316.6 jit_solution(4245026097874575158)
XLA Ops:
  7.2 12.5 %copy.22 = bf16[256,2,64,128]{0,3,2,1:T(8,128)(2,1)} copy(bf16[256,2,64,128]{3,2,1,0:T(8,128)(2,1)} %param.5) | data formatting | bytes 16777216 | tf_op args[0]
  19.8 34.2 %copy.23 = bf16[256,2,64,2,64]{4,3,2,1,0:T(2,128)(2,1)} copy(bf16[256,2,64,2,64]{0,4,3,2,1:T(8,128)(2,1)} %bitcast.36) | data formatting | bytes 16777216 | tf_op jit(solution)/shard_map/reshape | solution.py:16
  53.9 0.2 copy.21
  54.1 31.5 %convert_bitcast_fusion = bf16[256,2,64,4,64]{4,3,2,1,0:T(4,128)(2,1)} fusion(bf16[256,2,64,2,64]{4,3,2,1,0:T(2,128)(2,1)} %copy.23, s32[256,2,2]{2,1,0:T(2,128)S(1)} %copy.21), kind=kOutput, calls=%fused_computation | convolution fusion | flops 41947136 | bytes 25169920 | tf_op jit(solution)/shard_map/grsc,grisj->gricj/dot_general | solution.py:18
  85.6 49.5 %copy.24 = bf16[256,2,64,4,64]{0,4,3,2,1:T(8,128)(2,1)} copy(bf16[256,2,64,4,64]{4,3,2,1,0:T(4,128)(2,1)} %convert_bitcast_fusion) | data formatting | bytes 33554432 | tf_op jit(solution)/shard_map/convert_element_type | solution.py:19
  135.1 1.2 copy.27
  136.3 8.8 %convolution_convert_fusion.1 = bf16[256,32]{0,1:T(8,128)(2,1)S(1)} fusion(bf16[32,32768]{1,0:T(8,128)(2,1)S(1)} %bitcast.37, bf16[256,32768]{0,1:T(8,128)(2,1)} %bitcast.34), kind=kOutput, calls=%fused_computation.12 | convolution fusion | flops 536879104 | bytes 18890752 | tf_op jit(solution)/shard_map/dot_general | solution.py:29
  145.1 3.4 %psum.14 = bf16[256,32]{0,1:T(8,128)(2,1)S(1)} all-reduce(bf16[256,32]{0,1:T(8,128)(2,1)S(1)} %convolution_convert_fusion.1), channel_id=1, replica_groups=mesh['chol'=16,'walker'=8,'orb'=2] {'orb'}, use_global_device_ids=true, to_apply=%region_0.0 | all-reduce | flops 8192 | bytes 32768 | tf_op jit(solution)/shard_map/psum | solution.py:32
  148.4 12.7 %fusion.14 = f32[32,128,256]{2,0,1:T(8,128)} fusion(bf16[128,256,256]{2,1,0:T(8,128)(2,1)} %bitcast.35, f32[256,32]{0,1:T(8,128)S(1)} %copy-done.2, bf16[256,32]{0,1:T(8,128)(2,1)S(1)} %psum.14), kind=kOutput, calls=%fused_computation.23 | convolution fusion | flops 536895488 | bytes 21020672 | tf_op jit(solution)/shard_map/dot_general | solution.py:36
  161.1 6.6 %copy.25 = f32[32,128,256]{2,1,0:T(8,128)} copy(f32[32,128,256]{2,0,1:T(8,128)} %fusion.14) | data formatting | bytes 8388608 | tf_op jit(solution)/shard_map/dot_general | solution.py:36
  167.8 1.9 all_gather.15
  169.7 82.8 %reduce-scatter.2.cloned.1.call-done = f32[2,128,256]{2,1,0:T(8,128)} async-done(((f32[32,128,256]{2,1,0:T(8,128)}), f32[2,128,256]{2,1,0:T(8,128)}) %reduce-scatter.2.cloned.1.call-update) | async-done | bytes 262160 | tf_op jit(solution)/shard_map/reduce_scatter | solution.py:39
  252.5 1.0 multiply_convert_fusion
  253.5 0.2 convolution_convert_fusion
  253.7 1.9 all_gather.16
  255.6 0.2 fusion
  255.8 1.9 all_gather.17
  257.7 0.2 fusion.1
  257.8 1.9 all_gather.18
  259.7 0.8 fusion.6
  260.6 0.1 fusion.12
  260.7 38.8 %psum.15 = f32[32]{0:T(128)} all-reduce(f32[32]{0:T(128)S(1)} %broadcast_multiply_fusion), channel_id=1, replica_groups=mesh['chol'=16,'walker'=8,'orb'=2] {'chol'}, use_global_device_ids=true, to_apply=%region_3.0 | all-reduce | flops 32 | bytes 256 | tf_op jit(solution)/shard_map/psum | solution.py:33
  299.5 8.0 %all-gather.2.cloned.1.call-done = bf16[32,128,128]{2,1,0:T(8,128)(2,1)} async-done(((bf16[2,128,128]{2,1,0:T(8,128)(2,1)}), bf16[32,128,128]{2,1,0:T(8,128)(2,1)}) %all-gather.2.cloned.1.call-update) | async-done | bytes 1048592 | tf_op jit(solution)/shard_map/all_gather | solution.py:58
  307.5 2.3 copy.29
  (14 shorter events, 0.1 us)
Async XLA Ops:
  7.2 160.6 %copy-start = (bf16[32,128,128]{2,1,0:T(8,128)(2,1)S(1)}, bf16[32,128,128]{2,1,0:T(8,128)(2,1)}, u32[]{:S(2)}) copy-start(bf16[32,128,128]{2,1,0:T(8,128)(2,1)} %param.8) | copy-start | bytes 3145732
  7.2 245.3 %reduce-scatter.2.cloned.1.call-start = ((), (), s32[]{:S(2)}) async-start(), calls=%async_computation.1 | async-start | bytes 4456448 | tf_op jit(solution)/shard_map/reduce_scatter | solution.py:39
  19.7 34.2 %copy-start.3 = (s32[256,2,2]{0,2,1:T(2,128)S(1)}, s32[256,2,2]{0,2,1:T(2,128)}, u32[]{:S(2)}) copy-start(s32[256,2,2]{0,2,1:T(2,128)} %param.6) | copy-start | bytes 12292
  85.6 49.5 %copy-start.1 = (bf16[32,128,256]{2,1,0:T(8,128)(2,1)S(1)}, bf16[32,128,256]{2,1,0:T(8,128)(2,1)}, u32[]{:S(2)}) copy-start(bf16[32,128,256]{2,1,0:T(8,128)(2,1)} %param.7) | copy-start | bytes 6291460
  135.1 13.3 %copy-start.2 = (f32[256,32]{0,1:T(8,128)S(1)}, f32[256,32]{0,1:T(8,128)}, u32[]{:S(2)}) copy-start(f32[256,32]{0,1:T(8,128)} %param.9) | copy-start | bytes 98308
  167.7 139.8 %all-gather.2.cloned.1.call-start = ((), (), s32[]{:S(2)}) async-start(), calls=%async_computation.2 | async-start | bytes 1114112 | tf_op jit(solution)/shard_map/all_gather | solution.py:58
Sparse Core Ops, SparseCore 0:
  167.8 84.6 reduce-scatter.1
  260.7 46.7 all-gather.1
where the time goes:
time: 321 us; the launch traced here: 317 us
  local copies, waits for them, and re-layouts  106 us (33%)
  waiting for transfers between devices  90.9 us (28%)
  matrix products  54.3 us (17%)
  blocking collectives  49.8 us (16%)
  between operations  14.1 us (4%)
    reduce_scatter x1, waiting for transfers between devices, per_device(): lax.psum_scatter(summed.reshape(own_count * lax.axis_size('chol'), half_r...  82.8 us
    convert_element_type x1, local copies, waits for them, and re-layouts, dense_rows(): placed.astype(jnp.bfloat16).reshape(vectors, row_blocks * BLOCK * NORB)  49.5 us
    psum x1, blocking collectives, per_device(): energy = lax.psum(0.5 * jnp.sum(force_bias * force_bias, axis=0), 'chol')  38.8 us
    reshape x1, local copies, waits for them, and re-layouts, dense_rows(): pieces = values.reshape(vectors, row_blocks, BLOCK, SLOTS, BLOCK)  34.2 us
    dot_general x1, matrix products, dense_rows(): jnp.einsum('grsc,grisj->gricj', onehot, pieces, preferred_element_type=jn...  31.5 us
    unnamed x12, local copies, waits for them, and re-layouts  16.2 us
    dot_general x1, matrix products, per_device(): lax.dot_general(shifted, matrix, (((0,), (0,)), ((), ())), preferred_elem...  12.7 us
    dot_general x1, matrix products, per_device(): lax.dot_general(matrix, green_flat, (((1,), (1,)), ((), ())), preferred_e...  8.79 us
  transfers between devices with their start and end apart: 2, of which 2 were waited for; matrix products, arithmetic and copies ran while one was open for 0% of the time, Pallas kernels for 0%

commit v1 on v0

v1 whole, which is shorter than its diff:
```python
import functools

import jax
import jax.numpy as jnp
from jax import lax
from jax.experimental import pallas as pl
from jax.experimental.pallas import tpu as pltpu
from jax.sharding import PartitionSpec as P

NORB = 256
NOCC = 128
BLOCK = 64
TAYLOR = 4
SIDE = 4
F32 = jnp.float32
BF16 = jnp.bfloat16
MESH = pl.DeviceIdType.MESH
HALF = 64


def swap_halves(x):
    return jnp.concatenate([x[:, BLOCK:], x[:, :BLOCK]], axis=1)


def kernel(
    step_factor, v_hbm, cols_hbm, g_hbm, w_hbm, f_hbm, out_hbm, e_ref,
    vbuf, vt, gbuf, gp, cbuf, fbuf, wbuf, tbuf, fx, fxr,
    pp, opp1, fin1, s1, opp2, fin2, own2, pot, nw, gathered, esend, ebuf,
    lsem, ssem, rsem, osem,
):
    chip = lax.axis_index("chol")
    core = lax.axis_index("orb")
    other = 1 - core
    px, py = chip // SIDE, chip % SIDE

    def chip_at(dx, dy):
        return ((px + dx) % SIDE) * SIDE + (py + dy) % SIDE

    def chip_of(h, da, db):
        return chip_at(da, db) if h == 0 else chip_at(db, da)

    def walker(h, da, db):
        return 2 * chip_of(h, da, db) + h

    def dev(c, k):
        return {"chol": c, "orb": k}

    sends = []
    count = [0]

    def slots(n=1):
        count[0] += n
        return count[0] - n

    def remote(src, dst, to, sidx, ridx):
        return pltpu.make_async_remote_copy(
            src_ref=src, dst_ref=dst, send_sem=ssem.at[sidx], recv_sem=rsem.at[ridx],
            device_id=to, device_id_type=MESH,
        )

    def send(src, dst, to, ridx=None):
        sidx = slots()
        ridx = sidx if ridx is None else ridx
        c = remote(src, dst, to, sidx, ridx)
        c.start()
        sends.append(c)
        return ridx

    def arrive(dst, ridx):
        remote(dst, dst, dev(chip, other), ridx, ridx).wait_recv()

    barrier = pltpu.get_barrier_semaphore()
    partners = [dev(chip, other)]
    for dx, dy in ((1, 0), (3, 0), (0, 1), (0, 3)):
        partners += [dev(chip_at(dx, dy), core), dev(chip_at(dx, dy), other)]
    for dx, dy in ((2, 0), (0, 2)):
        partners.append(dev(chip_at(dx, dy), core))
    for to in partners:
        pl.semaphore_signal(barrier, inc=1, device_id=to, device_id_type=MESH)

    gcopy = pltpu.make_async_copy(g_hbm, gbuf, lsem.at[8])
    gcopy.start()
    vcopies = []
    for n in range(8):
        r, ii = divmod(n, 4)
        c = pltpu.make_async_copy(v_hbm.at[:, r, pl.ds(ii * 16, 16), :], vbuf.at[n], lsem.at[n])
        c.start()
        vcopies.append(c)
    fcopy = pltpu.make_async_copy(f_hbm, fbuf, lsem.at[9])
    fcopy.start()
    ccopy = pltpu.make_async_copy(cols_hbm, cbuf, lsem.at[10])
    ccopy.start()
    wcopy = pltpu.make_async_copy(w_hbm.at[pl.ds(2 * chip, 2)], wbuf, lsem.at[11])
    wcopy.start()

    gcopy.wait()
    low = lax.broadcasted_iota(jnp.int32, (16, 128), 1) < BLOCK
    own_at = pl.multiple_of(core * 128, 128)
    far_at = pl.multiple_of(other * 128, 128)
    for r in range(2):

        @pl.loop(0, 8)
        def _(n):
            w0 = pl.multiple_of((n % 2) * 16, 16)
            i0 = pl.multiple_of((n // 2) * 16, 16)
            rows = pl.ds(r * 64 + i0, 16)
            near = jnp.swapaxes(gbuf[pl.ds(w0, 16), rows, pl.ds(own_at, 128)], 0, 1)
            far = jnp.swapaxes(gbuf[pl.ds(w0, 16), rows, pl.ds(far_at, 128)], 0, 1)
            for i in range(16):
                a, b = near[i], far[i]
                if r == 1:
                    a = swap_halves(a)
                z = jnp.zeros_like(a)
                choices = (jnp.where(low, a, z), a, jnp.where(low, a, swap_halves(b)), jnp.where(low, a, b))
                for c, val in enumerate(choices):
                    gp[r, pl.ds(c * 32 + w0, 16), pl.ds(pl.multiple_of(i0 * 128, 128) + i * 128, 128)] = val

    acc = [None, None]
    for n in range(8):
        r, ii = divmod(n, 4)
        vcopies[n].wait()

        @pl.loop(0, 16)
        def _(gg):
            g0 = pl.multiple_of(gg * 16, 16)
            y = jnp.swapaxes(vbuf[n, pl.ds(g0, 16), :, :], 0, 1)
            for i in range(16):
                vt[r, pl.ds(g0, 16), (ii * 16 + i) * 128:(ii * 16 + i + 1) * 128] = y[i]

        ks = slice(ii * 2048, (ii + 1) * 2048)
        d = lax.dot_general(gp[r, :, ks], vt[r, :, ks], (((1,), (1,)), ((), ())), preferred_element_type=F32)
        acc[r] = d if acc[r] is None else acc[r] + d
    fcopy.wait()
    ccopy.wait()
    wcopy.wait()
    masks = []
    partial = jnp.zeros((32, 256), F32)
    for r in range(2):
        code = cbuf[r, 1:2, :]
        wanted = (4, 2 * core + (1 - r), 2 * other, 2 * other + 1)
        ms = [code == k for k in wanted]
        masks.append(ms)
        for c in range(4):
            partial = partial + jnp.where(ms[c], acc[r][c * 32:(c + 1) * 32], 0.0)
    fx[...] = partial
    tbuf[core] = wbuf[core]
    pl.semaphore_wait(barrier, len(partners))
    fi = send(fx, fxr, dev(chip, other))
    wi = send(wbuf.at[other], tbuf.at[core], dev(chip, other))
    arrive(fxr, fi)
    bias = partial + fxr[...]
    shifted = fbuf[...] - bias

    local = 0.5 * jnp.sum(bias * bias, axis=1, keepdims=True)
    diag = lax.broadcasted_iota(jnp.int32, (32, 128), 0) == lax.broadcasted_iota(jnp.int32, (32, 128), 1)
    row = jnp.sum(jnp.where(diag, local, 0.0), axis=0, keepdims=True)
    esend[0] = jnp.broadcast_to(row, (8, 128))
    ebuf[0, px] = jnp.broadcast_to(row, (8, 128))
    ex = slots(SIDE)
    for d in (1, 2, 3):
        send(esend.at[0], ebuf.at[0, px], dev(chip_at(d, 0), core), ex + px)

    lo32 = lax.broadcasted_iota(jnp.int32, (32, 128), 1) < BLOCK
    order = (2, 1, 3, 0)
    o1 = {}
    f1 = {}
    for r in range(2):
        parts = [shifted] + [jnp.where(masks[r][c], shifted, 0.0) for c in (1, 2, 3)]
        lhs = jnp.concatenate(parts, axis=0).astype(BF16)

        @pl.loop(0, 4)
        def _(ii):
            k0 = pl.multiple_of(ii * 2048, 2048)
            o = jnp.dot(lhs, vt[r, :, pl.ds(k0, 2048)], preferred_element_type=F32)
            x0, x1 = [], []
            for i in range(16):
                t = o[:, i * 128:(i + 1) * 128]
                x0.append(jnp.where(lo32, t[0:32], t[32:64]).astype(BF16))
                x1.append(jnp.where(lo32, pltpu.roll(t[64:96], 64, 1), t[96:128]).astype(BF16))
            i0 = pl.multiple_of(r * 64 + ii * 16, 16)
            for wh in range(2):
                for side, x in ((0, x0), (1, x1)):
                    s = jnp.stack([q[wh * 16:(wh + 1) * 16] for q in x], axis=0)
                    pp[wh * 16:(wh + 1) * 16, pl.ds(i0, 16), side * 128:(side + 1) * 128] = jnp.swapaxes(s, 0, 1)

        rows = pl.ds(r * HALF, HALF)
        step = 1 if r == 0 else 3
        for d in order:
            for h in range(2):
                o1[h, d, r] = send(pp.at[walker(h, 2, d), rows], opp1.at[h, d, r], dev(chip_of(h, step, 0), core))
        for d in order:
            for h in range(2):
                f1[h, d, 1 - r, r] = send(
                    pp.at[walker(h, 4 - step, d), rows], fin1.at[h, d, 1 - r, rows], dev(chip_of(h, 4 - step, 0), core)
                )

    for d in (1, 2, 3):
        qx = (px + d) % SIDE
        arrive(ebuf.at[0, qx], ex + qx)
    row = (ebuf[0, 0] + ebuf[0, 1]) + (ebuf[0, 2] + ebuf[0, 3])
    esend[1] = row
    ebuf[1, py] = row
    ey = slots(SIDE)
    for d in (1, 2, 3):
        send(esend.at[1], ebuf.at[1, py], dev(chip_at(0, d), core), ey + py)

    def forward1(d):
        for h in range(2):
            for r in range(2):
                rows = pl.ds(r * HALF, HALF)
                step = 1 if r == 0 else 3
                arrive(opp1.at[h, d, r], o1[h, d, r])
                w = walker(h, step, d)
                pp[w, rows] = (pp[w, rows].astype(F32) + opp1[h, d, r].astype(F32)).astype(BF16)
                f1[h, d, r, r] = send(pp.at[w, rows], fin1.at[h, d, r, rows], dev(chip_of(h, step, 0), core))

    def finish1(d):
        for h in range(2):
            for s in range(2):
                for r in range(2):
                    arrive(fin1.at[h, d, s, pl.ds(r * HALF, HALF)], f1[h, d, s, r])
            s1[h, d] = (
                pp[walker(h, 0, d)].astype(F32) + fin1[h, d, 0].astype(F32) + fin1[h, d, 1].astype(F32)
            ).astype(BF16)

    forward1(2)
    forward1(1)
    finish1(2)
    o2 = {}
    for h in range(2):
        for r in range(2):
            step = 1 if r == 0 else 3
            o2[h, r] = send(s1.at[h, 2, pl.ds(r * HALF, HALF)], opp2.at[h, r], dev(chip_of(h, 0, step), core))
    forward1(3)
    forward1(0)
    f2 = slots(8)
    for d, s in ((1, 0), (3, 1)):
        finish1(d)
        rows = pl.ds((1 - s) * HALF, HALF)
        for h in range(2):
            send(s1.at[h, d, rows], fin2.at[core, s, rows], dev(chip_of(h, 0, d), h), f2 + core * 4 + s * 2 + (1 - s))
    for d, s in ((1, 0), (3, 1)):
        rows = pl.ds(s * HALF, HALF)
        for h in range(2):
            arrive(opp2.at[h, s], o2[h, s])
            s1[h, d, rows] = (s1[h, d, rows].astype(F32) + opp2[h, s].astype(F32)).astype(BF16)
            send(s1.at[h, d, rows], fin2.at[core, s, rows], dev(chip_of(h, 0, d), h), f2 + core * 4 + s * 2 + s)
    finish1(0)
    own2[core] = s1[core, 0]
    oi = send(s1.at[other, 0], own2.at[core], dev(chip, other))

    for d in (1, 2, 3):
        qy = (py + d) % SIDE
        arrive(ebuf.at[1, qy], ey + qy)
    row = (ebuf[1, 0] + ebuf[1, 1]) + (ebuf[1, 2] + ebuf[1, 3])
    e_ref[...] = row[0:1, 0:32]

    arrive(own2.at[other], oi)
    for o in range(2):
        for s in range(2):
            for r in range(2):
                arrive(fin2.at[o, s, pl.ds(r * HALF, HALF)], f2 + o * 4 + s * 2 + r)
    for o in range(2):
        full = step_factor * (own2[o].astype(F32) + fin2[o, 0].astype(F32) + fin2[o, 1].astype(F32))
        near, far = full[:, :128], full[:, 128:]
        near = jnp.concatenate([near[:BLOCK], pltpu.roll(near[BLOCK:], BLOCK, 1)], axis=0)
        pair = [near, far] if o == 0 else [far, near]
        pot[o * 128:(o + 1) * 128, :] = jnp.concatenate(pair, axis=1).astype(BF16)
    arrive(tbuf.at[other], wi)
    start = tbuf[...].reshape(NORB, NOCC)
    term = start
    total = jnp.zeros((NORB, NOCC), F32)
    for degree in range(1, TAYLOR + 1):
        product = jnp.dot(pot[...], term, preferred_element_type=F32)
        term = (product / degree).astype(BF16)
        total = total + term.astype(F32)
    nw[...] = (start.astype(F32) + total).astype(BF16).reshape(2, 128, NOCC)

    mine = 2 * chip + core
    g1 = slots(4)
    for n, s in enumerate((1, 3)):
        for o in range(2):
            send(nw.at[o], gathered.at[mine], dev(chip_at(core * s, other * s), o), g1 + core * 2 + n)
    gi = send(nw.at[other], gathered.at[mine], dev(chip, other))
    gathered[mine] = nw[core]
    first, second = pl.ds(0, HALF), pl.ds(HALF, HALF)
    g2 = {}
    g3 = {}
    g4 = {}

    def done(w):
        pltpu.make_async_copy(gathered.at[w], out_hbm.at[w], osem).start()

    def spread(h, db):
        w = walker(h, 0, db)
        for n, step in enumerate((1, 3)):
            g3[h, db, n] = send(gathered.at[w], gathered.at[w], dev(chip_of(h, step, 0), core))
        done(w)

    arrive(gathered.at[2 * chip + other], gi)
    for h in range(2):
        spread(h, 0)
    for h in range(2):
        for n, (db, step, rows) in enumerate(((3, 1, first), (1, 3, second))):
            w = walker(h, 0, db)
            arrive(gathered.at[w], g1 + h * 2 + n)
            g2[h, n] = send(gathered.at[w, rows], gathered.at[w, rows], dev(chip_of(h, 0, step), core))
            spread(h, db)

    def pass_on(h, db):
        for n, (da, step, rows) in enumerate(((3, 1, first), (1, 3, second))):
            w = walker(h, da, db)
            arrive(gathered.at[w], g3[h, db, n])
            g4[h, db, n] = send(gathered.at[w, rows], gathered.at[w, rows], dev(chip_of(h, step, 0), core))
            done(w)

    for h in range(2):
        pass_on(h, 0)
    for h in range(2):
        for n, rows in enumerate((first, second)):
            arrive(gathered.at[walker(h, 0, 2), rows], g2[h, n])
        spread(h, 2)
    for db in (3, 1, 2):
        for h in range(2):
            pass_on(h, db)
    for db in (0, 3, 1, 2):
        for h in range(2):
            w = walker(h, 2, db)
            for n, rows in enumerate((first, second)):
                arrive(gathered.at[w, rows], g4[h, db, n])
            done(w)
    for c in sends:
        c.wait_send()
    pltpu.make_async_copy(gathered, out_hbm, osem).wait()
    assert count[0] <= SEMS, count[0]


SEMS = 160


def per_device(chol_vals, chol_cols, greens, walkers, fields):
    vectors = chol_vals.shape[0]
    step_factor = 72.0 / float(vectors * lax.axis_size("chol") * BLOCK) ** 0.5
    vmem = pltpu.VMEM
    any_space = pl.BlockSpec(memory_space=pl.ANY)
    new_walkers, energy = pl.pallas_call(
        functools.partial(kernel, step_factor),
        out_shape=(
            jax.ShapeDtypeStruct((32, 128, NOCC), BF16),
            jax.ShapeDtypeStruct((1, 32), F32),
        ),
        in_specs=[any_space] * 5,
        out_specs=(any_space, pl.BlockSpec(memory_space=vmem)),
        scratch_shapes=[
            vmem((8, 256, 16, 128), BF16),
            vmem((2, 256, 64 * 128), BF16),
            vmem((32, 128, 256), BF16),
            vmem((2, 128, 64 * 128), BF16),
            vmem((2, 2, 256), jnp.int32),
            vmem((32, 256), F32),
            vmem((2, 128, NOCC), BF16),
            vmem((2, 128, NOCC), BF16),
            vmem((32, 256), F32),
            vmem((32, 256), F32),
            vmem((32, 128, 256), BF16),
            vmem((2, 4, 2, HALF, 256), BF16),
            vmem((2, 4, 2, 128, 256), BF16),
            vmem((2, 4, 128, 256), BF16),
            vmem((2, 2, HALF, 256), BF16),
            vmem((2, 2, 128, 256), BF16),
            vmem((2, 128, 256), BF16),
            vmem((NORB, NORB), BF16),
            vmem((2, 128, NOCC), BF16),
            vmem((32, 128, NOCC), BF16),
            vmem((2, 8, 128), F32),
            vmem((2, SIDE, 8, 128), F32),
            pltpu.SemaphoreType.DMA((12,)),
            pltpu.SemaphoreType.DMA((SEMS,)),
            pltpu.SemaphoreType.DMA((SEMS,)),
            pltpu.SemaphoreType.DMA,
        ],
        compiler_params=pltpu.CompilerParams(
            collective_id=0, has_side_effects=True, vmem_limit_bytes=56 << 20
        ),
    )(chol_vals, chol_cols.transpose(1, 2, 0), greens, walkers, fields.T)
    return new_walkers, energy.reshape(32)


def solution(mesh):
    in_specs = (
        P("chol", "orb", None, None),
        P("chol", "orb", None),
        P("walker", "orb", None),
        P("walker", "orb", None),
        P("chol", "walker"),
    )
    out_specs = (P("walker", "orb", None), P("walker"))
    return jax.shard_map(
        per_device, mesh=mesh, in_specs=in_specs, out_specs=out_specs, check_vma=False
    )
```

time: 321 us -> 57.9 us (0.18); the launches traced: 317 us -> 57.7 us
  local copies, waits for them, and re-layouts: 106 us -> 3.42 us
  waiting for transfers between devices: 90.9 us -> 0 us
  matrix products: 54.3 us -> 0 us
  Pallas kernels: 0 us -> 53.7 us
  blocking collectives: 49.8 us -> 0 us
  between operations: 14.1 us -> 0.64 us
    reduce_scatter x1 -> x0, waiting for transfers between devices: 82.8 us -> none  [per_device(): lax.psum_scatter(summed.reshape(own_count * lax.axis_size('chol'), half_r...]
    dot_general x7 -> x0, matrix products: 54.3 us -> none  [the longest x1 31.5 us: dense_rows(): jnp.einsum('grsc,grisj->gricj', onehot, pieces, preferred_element_type=jn...]
    pallas_call x0 -> x1, Pallas kernels: none -> 53.7 us  [per_device(): pl.pallas_call(functools.partial(kernel, step_factor), out_shape=(jax.Sha...]
    convert_element_type x1 -> x0, local copies, waits for them, and re-layouts: 49.5 us -> none  [dense_rows(): placed.astype(jnp.bfloat16).reshape(vectors, row_blocks * BLOCK * NORB)]
    psum x2 -> x0, blocking collectives: 42.1 us -> none  [the longest x1 38.8 us: per_device(): energy = lax.psum(0.5 * jnp.sum(force_bias * force_bias, axis=0), 'chol')]
    reshape x1 -> x0, local copies, waits for them, and re-layouts: 34.2 us -> none  [dense_rows(): pieces = values.reshape(vectors, row_blocks, BLOCK, SLOTS, BLOCK)]
    unnamed x12 -> x2, local copies, waits for them, and re-layouts: 16.2 us -> 3.42 us
    all_gather x1 -> x0, waiting for transfers between devices: 7.99 us -> none  [per_device(): new_walkers = lax.all_gather(moved, 'chol', axis=0, tiled=True)]
  transfers between devices with their start and end apart: 2 -> 0, of which waited for: 2 -> 0; matrix products, arithmetic and copies ran while one was open for 0% -> 0% of each run, Pallas kernels for 0% -> 0%
where the time goes in v1:
time: 57.9 us; the launch traced here: 57.7 us
  Pallas kernels  53.7 us (93%)
  local copies, waits for them, and re-layouts  3.42 us (6%)
  between operations  0.64 us (1%)
    pallas_call x1, Pallas kernels, per_device(): pl.pallas_call(functools.partial(kernel, step_factor), out_shape=(jax.Sha...  53.7 us
    unnamed x2, local copies, waits for them, and re-layouts  3.42 us

profile of v1, /device:TPU:160, one launch (start us, length us, event | category | flops | bytes accessed | tf_op | source)
XLA Modules:
  0.0 57.7 jit_solution(3916797179011319420)
XLA Ops:
  0.6 53.7 %shard_map.68 = (bf16[32,128,128]{2,1,0:T(8,128)(2,1)}, f32[1,32]{1,0:T(1,128)}) custom-call(bf16[256,2,64,128]{3,2,1,0:T(8,128)(2,1)} %v_hbm.1, s32[2,2,256]{2,1,0:T(2,128)} %bitcast.4, bf16[32,128,256]{2,1,0:T(8,128)(2,1)} %g_hbm.1, bf16[32,128,128]{2,1,0:T(8,128)(2,1)} %w_hbm.1, f32[32,256]{1,0:T(8,128)} %bitcast.3), custom_call_target="tpu_custom_call" | custom-call | tf_op jit(solution)/shard_map/pallas_call | solution.py:346
  54.3 2.3 %copy.9 = bf16[32,128,128]{2,1,0:T(8,128)(2,1)} copy(bf16[32,128,128]{2,1,0:T(8,128)(2,1)} %get-tuple-element.8) | data formatting | bytes 2097152
  56.6 1.1 %copy.10 = f32[32]{0:T(128)} copy(f32[32]{0:T(128)} %bitcast.5) | data formatting | bytes 256

commit v2 on v0

v2 whole, which is shorter than its diff:
```python
import functools

import jax
import jax.numpy as jnp
from jax import lax
from jax.experimental import pallas as pl
from jax.experimental.pallas import tpu as pltpu
from jax.sharding import PartitionSpec as P

NORB = 256
NOCC = 128
BLOCK = 64
TAYLOR = 4
SIDE = 4
F32 = jnp.float32
BF16 = jnp.bfloat16
MESH = pl.DeviceIdType.MESH
HALF = 64


def swap_halves(x):
    return jnp.concatenate([x[:, BLOCK:], x[:, :BLOCK]], axis=1)


def kernel(
    step_factor, v_hbm, cols_hbm, g_hbm, w_hbm, f_hbm, out, e_ref,
    vbuf, vt, gbuf, gp, cbuf, fbuf, wbuf, tbuf, fx, fxr,
    pp, opp1, fin1, s1, last, pot, nw, esend, ebuf,
    lsem, ssem, rsem,
):
    chip = lax.axis_index("chol")
    core = lax.axis_index("orb")
    other = 1 - core
    px, py = chip // SIDE, chip % SIDE

    def chip_at(dx, dy):
        return ((px + dx) % SIDE) * SIDE + (py + dy) % SIDE

    def chip_of(h, da, db):
        return chip_at(da, db) if h == 0 else chip_at(db, da)

    def walker(h, da, db):
        return 2 * chip_of(h, da, db) + h

    def dev(c, k):
        return {"chol": c, "orb": k}

    used = [0]

    def slots(n=1):
        used[0] += n
        return used[0] - n

    def remote(src, dst, to, ridx, small=0):
        return pltpu.make_async_remote_copy(
            src_ref=src, dst_ref=dst, send_sem=ssem.at[small], recv_sem=rsem.at[ridx],
            device_id=to, device_id_type=MESH,
        )

    def send(src, dst, to, ridx, small=0):
        remote(src, dst, to, ridx, small).start()

    def arrive(dst, ridx):
        remote(dst, dst, dev(chip, other), ridx).wait_recv()

    barrier = pltpu.get_barrier_semaphore()
    partners = [dev(chip, other)]
    for dx, dy in ((1, 0), (3, 0), (2, 0), (0, 1), (0, 3), (0, 2)):
        partners += [dev(chip_at(dx, dy), core), dev(chip_at(dx, dy), other)]
    for to in partners:
        pl.semaphore_signal(barrier, inc=1, device_id=to, device_id_type=MESH)

    def load_g(n):
        rows = pl.ds(n * 16, 16)
        return pltpu.make_async_copy(g_hbm.at[:, rows, :], gbuf.at[:, rows, :], lsem.at[8 + n])

    def load_v(r, ii):
        n = r * 4 + ii
        return pltpu.make_async_copy(v_hbm.at[:, r, pl.ds(ii * 16, 16), :], vbuf.at[n], lsem.at[n])

    for r in range(2):
        for ii in range(4):
            load_g(r * 4 + ii).start()
            load_v(r, ii).start()
    fcopy = pltpu.make_async_copy(f_hbm, fbuf, lsem.at[16])
    fcopy.start()
    ccopy = pltpu.make_async_copy(cols_hbm, cbuf, lsem.at[17])
    ccopy.start()
    wcopy = pltpu.make_async_copy(w_hbm.at[pl.ds(2 * chip, 2)], wbuf, lsem.at[18])
    wcopy.start()

    low = lax.broadcasted_iota(jnp.int32, (16, 128), 1) < BLOCK
    own_at = pl.multiple_of(core * 128, 128)
    far_at = pl.multiple_of(other * 128, 128)
    for r in range(2):

        @pl.loop(0, 4)
        def _(ii):
            load_g(r * 4 + ii).wait()
            load_v(r, ii).wait()
            rows = pl.ds(pl.multiple_of(r * 64 + ii * 16, 16), 16)
            k0 = pl.multiple_of(ii * 2048, 2048)
            for w0 in (0, 16):
                near = jnp.swapaxes(gbuf[w0:w0 + 16, rows, pl.ds(own_at, 128)], 0, 1)
                far = jnp.swapaxes(gbuf[w0:w0 + 16, rows, pl.ds(far_at, 128)], 0, 1)
                for i in range(16):
                    a, b = near[i], far[i]
                    if r == 1:
                        a = swap_halves(a)
                    z = jnp.zeros_like(a)
                    choices = (jnp.where(low, a, z), a, jnp.where(low, a, swap_halves(b)), jnp.where(low, a, b))
                    for c, val in enumerate(choices):
                        gp[r, c * 32 + w0:c * 32 + w0 + 16, pl.ds(k0 + i * 128, 128)] = val
            for g0 in range(0, 256, 16):
                y = jnp.swapaxes(vbuf[r * 4 + ii, g0:g0 + 16, :, :], 0, 1)
                for i in range(16):
                    vt[r, g0:g0 + 16, pl.ds(k0 + i * 128, 128)] = y[i]

    fcopy.wait()
    ccopy.wait()
    wcopy.wait()
    masks = []
    partial = jnp.zeros((32, 256), F32)
    for r in range(2):
        acc = lax.dot_general(vt[r], gp[r], (((1,), (1,)), ((), ())), preferred_element_type=F32).T
        code = cbuf[r, 1:2, :]
        wanted = (4, 2 * core + (1 - r), 2 * other, 2 * other + 1)
        ms = [code == k for k in wanted]
        masks.append(ms)
        for c in range(4):
            partial = partial + jnp.where(ms[c], acc[c * 32:(c + 1) * 32], 0.0)
    fx[...] = partial
    tbuf[core] = wbuf[core]
    fi, wi = slots(), slots()
    pl.semaphore_wait(barrier, len(partners))
    send(fx, fxr, dev(chip, other), fi)
    send(wbuf.at[other], tbuf.at[core], dev(chip, other), wi)
    arrive(fxr, fi)
    bias = partial + fxr[...]
    shifted = fbuf[...] - bias

    local = 0.5 * jnp.sum(bias * bias, axis=1, keepdims=True)
    diag = lax.broadcasted_iota(jnp.int32, (32, 128), 0) == lax.broadcasted_iota(jnp.int32, (32, 128), 1)
    row = jnp.sum(jnp.where(diag, local, 0.0), axis=0, keepdims=True)
    esend[0] = jnp.broadcast_to(row, (8, 128))
    ex, ey = slots(), slots()
    for d in (1, 2, 3):
        send(esend.at[0], ebuf.at[0, d], dev(chip_at(d, 0), core), ex, 1)

    lo32 = lax.broadcasted_iota(jnp.int32, (32, 128), 1) < BLOCK
    order = (2, 1, 3, 0)
    o1 = {(h, d, r): slots() for h in range(2) for d in range(4) for r in range(2)}
    f1 = {(h, d): slots() for h in range(2) for d in (1, 2, 3)}
    fl = slots()

    def rows_of(r):
        return pl.ds(r * HALF, HALF)

    def way(r):
        return 1 if r == 0 else 3

    def send_opp(d, r):
        for h in range(2):
            send(pp.at[walker(h, 2, d), rows_of(r)], opp1.at[h, d, r], dev(chip_of(h, way(r), 0), core), o1[h, d, r])

    def send_target(d, r, step):
        s = 0 if step == 1 else 1
        for h in range(2):
            src = pp.at[walker(h, step, d), rows_of(r)]
            if d == 0:
                send(src, last.at[core * 5 + s, rows_of(r)], dev(chip_of(h, step, 0), h), fl)
            else:
                send(src, fin1.at[h, d, s, rows_of(r)], dev(chip_of(h, step, 0), core), f1[h, d])

    def add_opp(d, r):
        for h in range(2):
            arrive(opp1.at[h, d, r], o1[h, d, r])
            w = walker(h, way(r), d)
            pp[w, rows_of(r)] = (pp[w, rows_of(r)].astype(F32) + opp1[h, d, r].astype(F32)).astype(BF16)

    for r in range(2):
        parts = [shifted] + [jnp.where(masks[r][c], shifted, 0.0) for c in (1, 2, 3)]
        lhs = jnp.concatenate(parts, axis=0).astype(BF16)

        @pl.loop(0, 4)
        def _(ii):
            k0 = pl.multiple_of(ii * 2048, 2048)
            o = jnp.dot(lhs, vt[r, :, pl.ds(k0, 2048)], preferred_element_type=F32)
            x0, x1 = [], []
            for i in range(16):
                t = o[:, i * 128:(i + 1) * 128]
                x0.append(jnp.where(lo32, t[0:32], t[32:64]).astype(BF16))
                x1.append(jnp.where(lo32, pltpu.roll(t[64:96], 64, 1), t[96:128]).astype(BF16))
            i0 = pl.multiple_of(r * 64 + ii * 16, 16)
            for wh in range(2):
                for side, x in ((0, x0), (1, x1)):
                    s = jnp.stack([q[wh * 16:(wh + 1) * 16] for q in x], axis=0)
                    pp[wh * 16:(wh + 1) * 16, pl.ds(i0, 16), side * 128:(side + 1) * 128] = jnp.swapaxes(s, 0, 1)

        for d in order:
            send_opp(d, r)
        if r == 0:
            send_target(2, 0, 3)
            send_target(1, 0, 3)
    send_target(2, 1, 1)
    send_target(1, 1, 1)
    send(pp.at[2 * chip + other], last.at[10], dev(chip, other), fl)

    arrive(ebuf.at[0, pl.ds(1, 3)], ex)
    ebuf[0, 0] = esend[0]
    row = ordered_sum(ebuf, 0, px)
    esend[1] = row
    for d in (1, 2, 3):
        send(esend.at[1], ebuf.at[1, d], dev(chip_at(0, d), core), ey, 1)

    for n, d in enumerate(order):
        for r in range(2):
            add_opp(d, r)
            send_target(d, r, way(r))
        if n + 2 < 4:
            send_target(order[n + 2], 1, 1)
            send_target(order[n + 2], 0, 3)
    for d in (2, 1, 3):
        for h in range(2):
            arrive(fin1.at[h, d], f1[h, d])
            s1[h, d] = (
                pp[walker(h, 0, d)].astype(F32) + fin1[h, d, 0].astype(F32) + fin1[h, d, 1].astype(F32)
            ).astype(BF16)
            send(s1.at[h, d], last.at[core * 5 + 1 + d], dev(chip_of(h, 0, d), h), fl)

    arrive(ebuf.at[1, pl.ds(1, 3)], ey)
    ebuf[1, 0] = esend[1]
    row = ordered_sum(ebuf, 1, py)
    e_ref[...] = row[0:1, 0:32]

    mine = 2 * chip + core
    arrive(last, fl)
    for o in range(2):
        own = jnp.where(core == o, pp[mine].astype(F32), last[10].astype(F32))
        for n in range(5):
            own = own + last[o * 5 + n].astype(F32)
        full = step_factor * own
        near, far = full[:, :128], full[:, 128:]
        near = jnp.concatenate([near[:BLOCK], pltpu.roll(near[BLOCK:], BLOCK, 1)], axis=0)
        pair = [near, far] if o == 0 else [far, near]
        pot[o * 128:(o + 1) * 128, :] = jnp.concatenate(pair, axis=1).astype(BF16)
    arrive(tbuf.at[other], wi)
    start = tbuf[...].reshape(NORB, NOCC)
    term = start
    total = jnp.zeros((NORB, NOCC), F32)
    for degree in range(1, TAYLOR + 1):
        product = jnp.dot(pot[...], term, preferred_element_type=F32)
        term = (product / degree).astype(BF16)
        total = total + term.astype(F32)
    nw[...] = (start.astype(F32) + total).astype(BF16).reshape(2, 128, NOCC)

    g1 = slots(6)
    g2 = slots()
    for d in (2, 1, 3):
        for o in range(2):
            send(nw.at[o], out.at[mine], dev(chip_at(core * d, other * d), o), g1 + core * 3 + d - 1)
    for d in (2, 1, 3):
        for o in range(2):
            send(nw.at[o], out.at[mine], dev(chip_at(other * d, core * d), o), g2)
    send(nw.at[other], out.at[mine], dev(chip, other), g2)
    keep = pltpu.make_async_copy(nw.at[core], out.at[mine], lsem.at[0])
    keep.start()
    for d in (1, 3, 2):
        for h in range(2):
            w = walker(h, 0, 4 - d)
            arrive(out.at[w], g1 + h * 3 + d - 1)
            for da in (2, 1, 3):
                send(out.at[w], out.at[w], dev(chip_of(h, da, 0), core), g2)
    keep.wait()
    arrive(out.at[pl.ds(0, 25)], g2)
    whole = pl.ds(0, 190)
    pltpu.make_async_copy(vbuf.at[pl.ds(0, 4), whole], vbuf.at[pl.ds(4, 4), whole], ssem.at[0]).wait()
    pltpu.make_async_copy(ebuf.at[:, pl.ds(0, 3)], ebuf.at[:, pl.ds(1, 3)], ssem.at[1]).wait()
    assert used[0] == SEMS, used[0]


def ordered_sum(ebuf, stage, at):
    rows = [ebuf[stage, (at - q + SIDE) % SIDE] for q in range(SIDE)]
    return (rows[0] + rows[1]) + (rows[2] + rows[3])


SEMS = 34


def per_device(chol_vals, chol_cols, greens, walkers, fields):
    vectors = chol_vals.shape[0]
    step_factor = 72.0 / float(vectors * lax.axis_size("chol") * BLOCK) ** 0.5
    vmem = pltpu.VMEM
    hbm = pl.BlockSpec(memory_space=pltpu.HBM)
    new_walkers, energy = pl.pallas_call(
        functools.partial(kernel, step_factor),
        out_shape=(
            jax.ShapeDtypeStruct((32, 128, NOCC), BF16),
            jax.ShapeDtypeStruct((1, 32), F32),
        ),
        in_specs=[hbm] * 5,
        out_specs=(pl.BlockSpec(memory_space=pl.ANY), pl.BlockSpec(memory_space=vmem)),
        scratch_shapes=[
            vmem((8, 256, 16, 128), BF16),
            vmem((2, 256, 64 * 128), BF16),
            vmem((32, 128, 256), BF16),
            vmem((2, 128, 64 * 128), BF16),
            vmem((2, 2, 256), jnp.int32),
            vmem((32, 256), F32),
            vmem((2, 128, NOCC), BF16),
            vmem((2, 128, NOCC), BF16),
            vmem((32, 256), F32),
            vmem((32, 256), F32),
            vmem((32, 128, 256), BF16),
            vmem((2, 4, 2, HALF, 256), BF16),
            vmem((2, 4, 2, 128, 256), BF16),
            vmem((2, 4, 128, 256), BF16),
            vmem((11, 128, 256), BF16),
            vmem((NORB, NORB), BF16),
            vmem((2, 128, NOCC), BF16),
            vmem((2, 8, 128), F32),
            vmem((2, SIDE, 8, 128), F32),
            pltpu.SemaphoreType.DMA((19,)),
            pltpu.SemaphoreType.DMA((2,)),
            pltpu.SemaphoreType.DMA((SEMS,)),
        ],
        compiler_params=pltpu.CompilerParams(
            collective_id=0, has_side_effects=True, vmem_limit_bytes=44 << 20
        ),
    )(*[pltpu.with_memory_space_constraint(a, pltpu.HBM) for a in (chol_vals, chol_cols.transpose(1, 2, 0), greens, walkers, fields.T)])
    return new_walkers, energy.reshape(32)


def solution(mesh):
    in_specs = (
        P("chol", "orb", None, None),
        P("chol", "orb", None),
        P("walker", "orb", None),
        P("walker", "orb", None),
        P("chol", "walker"),
    )
    out_specs = (P("walker", "orb", None), P("walker"))
    return jax.shard_map(
        per_device, mesh=mesh, in_specs=in_specs, out_specs=out_specs, check_vma=False
    )
```

time: 321 us -> 44.6 us (0.14)
  the two profiles are of different devices: /device:TPU:160 before, /device:TPU:1 now
where the time goes in v2:
time: 44.6 us
  Pallas kernels  42.4 us (95%)
  local copies, waits for them, and re-layouts  1.48 us (3%)
  between operations  0.64 us (1%)
    pallas_call x1, Pallas kernels, per_device(): pl.pallas_call(functools.partial(kernel, step_factor), out_shape=(jax.Sha...  42.4 us
    unnamed x2, local copies, waits for them, and re-layouts  1.48 us

profile of v2, /device:TPU:1, one launch (start us, length us, event | category | flops | bytes accessed | tf_op | source)
XLA Modules:
  0.0 44.6 jit_solution(13252346357714774519)
XLA Ops:
  0.6 42.4 %shard_map.68 = (bf16[32,128,128]{2,1,0:T(8,128)(2,1)S(1)}, f32[1,32]{1,0:T(1,128)S(1)}) custom-call(bf16[256,2,64,128]{3,2,1,0:T(8,128)(2,1)} %v_hbm.1, s32[2,2,256]{2,1,0:T(2,128)} %bitcast.5, bf16[32,128,256]{2,1,0:T(8,128)(2,1)} %g_hbm.1, bf16[32,128,128]{2,1,0:T(8,128)(2,1)} %w_hbm.1, f32[32,256]{1,0:T(8,128)} %bitcast.4), custom_call_target="tpu_custom_call" | custom-call | tf_op jit(solution)/shard_map/pallas_call | solution.py:295
  43.1 1.0 %copy.9 = bf16[32,128,128]{2,1,0:T(8,128)(2,1)} copy(bf16[32,128,128]{2,1,0:T(8,128)(2,1)S(1)} %get-tuple-element.8) | data formatting | bytes 2097152
  44.0 0.5 %copy.10 = f32[32]{0:T(128)} copy(f32[32]{0:T(128)S(1)} %bitcast.3) | data formatting | bytes 256

commit v3 on v2

--- a/solution.py
+++ b/solution.py
@@ -16,6 +16,7 @@
 BF16 = jnp.bfloat16
 MESH = pl.DeviceIdType.MESH
 HALF = 64
+WAY = (1, 3)
 
 
 def swap_halves(x):
@@ -153,37 +154,40 @@
     f1 = {(h, d): slots() for h in range(2) for d in (1, 2, 3)}
     fl = slots()
 
-    def rows_of(r):
-        return pl.ds(r * HALF, HALF)
-
-    def way(r):
-        return 1 if r == 0 else 3
-
-    def send_opp(d, r):
-        for h in range(2):
-            send(pp.at[walker(h, 2, d), rows_of(r)], opp1.at[h, d, r], dev(chip_of(h, way(r), 0), core), o1[h, d, r])
-
-    def send_target(d, r, step):
-        s = 0 if step == 1 else 1
-        for h in range(2):
-            src = pp.at[walker(h, step, d), rows_of(r)]
+    def rows_of(r, q):
+        return pl.ds(r * HALF + q * 32, 32)
+
+    def send_opp(d, r, q):
+        for h in range(2):
+            src = pp.at[walker(h, 2, d), rows_of(r, q)]
+            send(src, opp1.at[h, d, r, q], dev(chip_of(h, WAY[q], 0), core), o1[h, d, r])
+
+    def send_target(d, r, q, s):
+        for h in range(2):
+            src = pp.at[walker(h, WAY[s], d), rows_of(r, q)]
             if d == 0:
-                send(src, last.at[core * 5 + s, rows_of(r)], dev(chip_of(h, step, 0), h), fl)
+                send(src, last.at[core * 5 + s, rows_of(r, q)], dev(chip_of(h, WAY[s], 0), h), fl)
             else:
-                send(src, fin1.at[h, d, s, rows_of(r)], dev(chip_of(h, step, 0), core), f1[h, d])
+                send(src, fin1.at[h, d, s, rows_of(r, q)], dev(chip_of(h, WAY[s], 0), core), f1[h, d])
+
+    def send_own(d, r):
+        for s in range(2):
+            send_target(d, r, 1 - s, s)
 
     def add_opp(d, r):
         for h in range(2):
             arrive(opp1.at[h, d, r], o1[h, d, r])
-            w = walker(h, way(r), d)
-            pp[w, rows_of(r)] = (pp[w, rows_of(r)].astype(F32) + opp1[h, d, r].astype(F32)).astype(BF16)
+            for q in range(2):
+                w = walker(h, WAY[q], d)
+                pp[w, rows_of(r, q)] = (pp[w, rows_of(r, q)].astype(F32) + opp1[h, d, r, q].astype(F32)).astype(BF16)
+        for s in range(2):
+            send_target(d, r, s, s)
 
     for r in range(2):
         parts = [shifted] + [jnp.where(masks[r][c], shifted, 0.0) for c in (1, 2, 3)]
         lhs = jnp.concatenate(parts, axis=0).astype(BF16)
 
-        @pl.loop(0, 4)
-        def _(ii):
+        def part(ii):
             k0 = pl.multiple_of(ii * 2048, 2048)
             o = jnp.dot(lhs, vt[r, :, pl.ds(k0, 2048)], preferred_element_type=F32)
             x0, x1 = [], []
@@ -197,13 +201,13 @@
                     s = jnp.stack([q[wh * 16:(wh + 1) * 16] for q in x], axis=0)
                     pp[wh * 16:(wh + 1) * 16, pl.ds(i0, 16), side * 128:(side + 1) * 128] = jnp.swapaxes(s, 0, 1)
 
-        for d in order:
-            send_opp(d, r)
+        for q in range(2):
+            pl.loop(2 * q, 2 * q + 2)(part)
+            for d in order:
+                send_opp(d, r, q)
         if r == 0:
-            send_target(2, 0, 3)
-            send_target(1, 0, 3)
-    send_target(2, 1, 1)
-    send_target(1, 1, 1)
+            send_own(2, 0)
+            send_own(1, 0)
     send(pp.at[2 * chip + other], last.at[10], dev(chip, other), fl)
 
     arrive(ebuf.at[0, pl.ds(1, 3)], ex)
@@ -213,13 +217,17 @@
     for d in (1, 2, 3):
         send(esend.at[1], ebuf.at[1, d], dev(chip_at(0, d), core), ey, 1)
 
-    for n, d in enumerate(order):
+    send_own(2, 1)
+    add_opp(2, 0)
+    add_opp(1, 0)
+    send_own(1, 1)
+    add_opp(2, 1)
+    add_opp(1, 1)
+    for d in (3, 0):
+        for r in range(2):
+            send_own(d, r)
         for r in range(2):
             add_opp(d, r)
-            send_target(d, r, way(r))
-        if n + 2 < 4:
-            send_target(order[n + 2], 1, 1)
-            send_target(order[n + 2], 0, 3)
     for d in (2, 1, 3):
         for h in range(2):
             arrive(fin1.at[h, d], f1[h, d])
@@ -258,13 +266,15 @@
     g2 = slots()
     for d in (2, 1, 3):
         for o in range(2):
-            send(nw.at[o], out.at[mine], dev(chip_at(core * d, other * d), o), g1 + core * 3 + d - 1)
+            send(nw.at[o], out.at[mine], dev(chip_at(core * d, other * d), o), g1 + core * 3 + d - 1, 2)
+    send(nw.at[other], out.at[mine], dev(chip, other), g2)
+    keep = pltpu.make_async_copy(nw.at[core], out.at[mine], lsem.at[0])
+    keep.start()
+    sent_first = pl.ds(0, 48)
+    pltpu.make_async_copy(vbuf.at[0, sent_first], vbuf.at[1, sent_first], ssem.at[2]).wait()
     for d in (2, 1, 3):
         for o in range(2):
             send(nw.at[o], out.at[mine], dev(chip_at(other * d, core * d), o), g2)
-    send(nw.at[other], out.at[mine], dev(chip, other), g2)
-    keep = pltpu.make_async_copy(nw.at[core], out.at[mine], lsem.at[0])
-    keep.start()
     for d in (1, 3, 2):
         for h in range(2):
             w = walker(h, 0, 4 - d)
@@ -273,7 +283,7 @@
                 send(out.at[w], out.at[w], dev(chip_of(h, da, 0), core), g2)
     keep.wait()
     arrive(out.at[pl.ds(0, 25)], g2)
-    whole = pl.ds(0, 190)
+    whole = pl.ds(0, 178)
     pltpu.make_async_copy(vbuf.at[pl.ds(0, 4), whole], vbuf.at[pl.ds(4, 4), whole], ssem.at[0]).wait()
     pltpu.make_async_copy(ebuf.at[:, pl.ds(0, 3)], ebuf.at[:, pl.ds(1, 3)], ssem.at[1]).wait()
     assert used[0] == SEMS, used[0]
@@ -285,6 +295,17 @@
 
 
 SEMS = 34
+
+
+def write_out(w_ref, e_ref, w_out, e_out, sem):
+    copies = [
+        pltpu.make_async_copy(w_ref, w_out, sem.at[0]),
+        pltpu.make_async_copy(e_ref, e_out, sem.at[1]),
+    ]
+    for c in copies:
+        c.start()
+    for c in copies:
+        c.wait()
 
 
 def per_device(chol_vals, chol_cols, greens, walkers, fields):
@@ -312,7 +333,7 @@
             vmem((32, 256), F32),
             vmem((32, 256), F32),
             vmem((32, 128, 256), BF16),
-            vmem((2, 4, 2, HALF, 256), BF16),
+            vmem((2, 4, 2, 2, 32, 256), BF16),
             vmem((2, 4, 2, 128, 256), BF16),
             vmem((2, 4, 128, 256), BF16),
             vmem((11, 128, 256), BF16),
@@ -321,13 +342,25 @@
             vmem((2, 8, 128), F32),
             vmem((2, SIDE, 8, 128), F32),
             pltpu.SemaphoreType.DMA((19,)),
-            pltpu.SemaphoreType.DMA((2,)),
+            pltpu.SemaphoreType.DMA((3,)),
             pltpu.SemaphoreType.DMA((SEMS,)),
         ],
         compiler_params=pltpu.CompilerParams(
             collective_id=0, has_side_effects=True, vmem_limit_bytes=44 << 20
         ),
     )(*[pltpu.with_memory_space_constraint(a, pltpu.HBM) for a in (chol_vals, chol_cols.transpose(1, 2, 0), greens, walkers, fields.T)])
+    in_vmem = pl.BlockSpec(memory_space=pl.ANY)
+    new_walkers, energy = pl.pallas_call(
+        write_out,
+        out_shape=(
+            jax.ShapeDtypeStruct((32, 128, NOCC), BF16),
+            jax.ShapeDtypeStruct((1, 32), F32),
+        ),
+        in_specs=[in_vmem, in_vmem],
+        out_specs=(hbm, hbm),
+        scratch_shapes=[pltpu.SemaphoreType.DMA((2,))],
+        compiler_params=pltpu.CompilerParams(vmem_limit_bytes=8 << 20),
+    )(new_walkers, energy)
     return new_walkers, energy.reshape(32)
 
 

time: 44.6 us -> 43 us (0.964)
  the two profiles are of different devices: /device:TPU:1 before, /device:TPU:160 now
where the time goes in v3:
time: 43 us; the launch traced here: 42.9 us
  Pallas kernels  42.3 us (98%)
  between operations  0.64 us (1%)
    pallas_call x1, Pallas kernels, per_device(): pl.pallas_call(functools.partial(kernel, step_factor), out_shape=(jax.Sha...  41.3 us
    pallas_call x1, Pallas kernels, per_device(): pl.pallas_call(write_out, out_shape=(jax.ShapeDtypeStruct((32, 128, NOCC)...  0.99 us

profile of v3, /device:TPU:160, one launch (start us, length us, event | category | flops | bytes accessed | tf_op | source)
XLA Modules:
  0.0 42.9 jit_solution(14456383097734249672)
XLA Ops:
  0.6 41.3 %shard_map.68 = (bf16[32,128,128]{2,1,0:T(8,128)(2,1)S(1)}, f32[1,32]{1,0:T(1,128)S(1)}) custom-call(bf16[256,2,64,128]{3,2,1,0:T(8,128)(2,1)} %v_hbm.1, s32[2,2,256]{2,1,0:T(2,128)} %bitcast.4, bf16[32,128,256]{2,1,0:T(8,128)(2,1)} %g_hbm.1, bf16[32,128,128]{2,1,0:T(8,128)(2,1)} %w_hbm.1, f32[32,256]{1,0:T(8,128)} %bitcast.3), custom_call_target="tpu_custom_call" | custom-call | tf_op jit(solution)/shard_map/pallas_call | solution.py:316
  41.9 1.0 %shard_map.69 = (bf16[32,128,128]{2,1,0:T(8,128)(2,1)}, f32[1,32]{1,0:T(1,128)}) custom-call(bf16[32,128,128]{2,1,0:T(8,128)(2,1)S(1)} %get-tuple-element.6.w_ref, f32[1,32]{1,0:T(1,128)S(1)} %get-tuple-element.7.e_ref), custom_call_target="tpu_custom_call" | custom-call | tf_op jit(solution)/shard_map/pallas_call | solution.py:353

commit v4 on v3

--- a/solution.py
+++ b/solution.py
@@ -149,9 +149,8 @@
         send(esend.at[0], ebuf.at[0, d], dev(chip_at(d, 0), core), ex, 1)
 
     lo32 = lax.broadcasted_iota(jnp.int32, (32, 128), 1) < BLOCK
-    order = (2, 1, 3, 0)
     o1 = {(h, d, r): slots() for h in range(2) for d in range(4) for r in range(2)}
-    f1 = {(h, d): slots() for h in range(2) for d in (1, 2, 3)}
+    f1 = {(h, d, r): slots() for h in range(2) for d in (1, 2, 3) for r in range(2)}
     fl = slots()
 
     def rows_of(r, q):
@@ -168,7 +167,7 @@
             if d == 0:
                 send(src, last.at[core * 5 + s, rows_of(r, q)], dev(chip_of(h, WAY[s], 0), h), fl)
             else:
-                send(src, fin1.at[h, d, s, rows_of(r, q)], dev(chip_of(h, WAY[s], 0), core), f1[h, d])
+                send(src, fin1.at[h, d, r, s, q], dev(chip_of(h, WAY[s], 0), core), f1[h, d, r])
 
     def send_own(d, r):
         for s in range(2):
@@ -203,11 +202,10 @@
 
         for q in range(2):
             pl.loop(2 * q, 2 * q + 2)(part)
-            for d in order:
+            for d in (2, 1, 3) if r else (2, 1, 3, 0):
                 send_opp(d, r, q)
-        if r == 0:
-            send_own(2, 0)
-            send_own(1, 0)
+        for d in (2, 1) if r else (2, 1, 3, 0):
+            send_own(d, r)
     send(pp.at[2 * chip + other], last.at[10], dev(chip, other), fl)
 
     arrive(ebuf.at[0, pl.ds(1, 3)], ex)
@@ -217,24 +215,28 @@
     for d in (1, 2, 3):
         send(esend.at[1], ebuf.at[1, d], dev(chip_at(0, d), core), ey, 1)
 
-    send_own(2, 1)
-    add_opp(2, 0)
-    add_opp(1, 0)
-    send_own(1, 1)
-    add_opp(2, 1)
-    add_opp(1, 1)
-    for d in (3, 0):
-        for r in range(2):
-            send_own(d, r)
-        for r in range(2):
-            add_opp(d, r)
-    for d in (2, 1, 3):
-        for h in range(2):
-            arrive(fin1.at[h, d], f1[h, d])
-            s1[h, d] = (
-                pp[walker(h, 0, d)].astype(F32) + fin1[h, d, 0].astype(F32) + fin1[h, d, 1].astype(F32)
-            ).astype(BF16)
-            send(s1.at[h, d], last.at[core * 5 + 1 + d], dev(chip_of(h, 0, d), h), fl)
+    def finish(d, r):
+        rows = pl.ds(r * HALF, HALF)
+        for h in range(2):
+            arrive(fin1.at[h, d, r], f1[h, d, r])
+            both = fin1[h, d, r, 0].astype(F32) + fin1[h, d, r, 1].astype(F32)
+            s1[h, d, r] = (pp[walker(h, 0, d), rows].astype(F32) + both.reshape(HALF, 256)).astype(BF16)
+            send(s1.at[h, d, r], last.at[core * 5 + 1 + d, rows], dev(chip_of(h, 0, d), h), fl)
+
+    for d in (2, 1, 3):
+        add_opp(d, 0)
+    send_own(3, 1)
+    add_opp(0, 0)
+    for q in range(2):
+        send_opp(0, 1, q)
+    send_own(0, 1)
+    for d in (2, 1, 3):
+        add_opp(d, 1)
+    for d in (2, 1, 3):
+        finish(d, 0)
+    add_opp(0, 1)
+    for d in (2, 1, 3):
+        finish(d, 1)
 
     arrive(ebuf.at[1, pl.ds(1, 3)], ey)
     ebuf[1, 0] = esend[1]
@@ -264,13 +266,14 @@
 
     g1 = slots(6)
     g2 = slots()
-    for d in (2, 1, 3):
+    for d in (1, 3, 2):
         for o in range(2):
-            send(nw.at[o], out.at[mine], dev(chip_at(core * d, other * d), o), g1 + core * 3 + d - 1, 2)
+            to = dev(chip_at(core * d, other * d), o)
+            send(nw.at[o], out.at[mine], to, g1 + core * 3 + d - 1, 0 if d == 2 else 2)
     send(nw.at[other], out.at[mine], dev(chip, other), g2)
     keep = pltpu.make_async_copy(nw.at[core], out.at[mine], lsem.at[0])
     keep.start()
-    sent_first = pl.ds(0, 48)
+    sent_first = pl.ds(0, 32)
     pltpu.make_async_copy(vbuf.at[0, sent_first], vbuf.at[1, sent_first], ssem.at[2]).wait()
     for d in (2, 1, 3):
         for o in range(2):
@@ -283,7 +286,7 @@
                 send(out.at[w], out.at[w], dev(chip_of(h, da, 0), core), g2)
     keep.wait()
     arrive(out.at[pl.ds(0, 25)], g2)
-    whole = pl.ds(0, 178)
+    whole = pl.ds(0, 182)
     pltpu.make_async_copy(vbuf.at[pl.ds(0, 4), whole], vbuf.at[pl.ds(4, 4), whole], ssem.at[0]).wait()
     pltpu.make_async_copy(ebuf.at[:, pl.ds(0, 3)], ebuf.at[:, pl.ds(1, 3)], ssem.at[1]).wait()
     assert used[0] == SEMS, used[0]
@@ -294,7 +297,7 @@
     return (rows[0] + rows[1]) + (rows[2] + rows[3])
 
 
-SEMS = 34
+SEMS = 40
 
 
 def write_out(w_ref, e_ref, w_out, e_out, sem):
@@ -334,8 +337,8 @@
             vmem((32, 256), F32),
             vmem((32, 128, 256), BF16),
             vmem((2, 4, 2, 2, 32, 256), BF16),
-            vmem((2, 4, 2, 128, 256), BF16),
-            vmem((2, 4, 128, 256), BF16),
+            vmem((2, 4, 2, 2, 2, 32, 256), BF16),
+            vmem((2, 4, 2, HALF, 256), BF16),
             vmem((11, 128, 256), BF16),
             vmem((NORB, NORB), BF16),
             vmem((2, 128, NOCC), BF16),

time: 43 us -> 42.1 us (0.979)
  Pallas kernels: 42.3 us -> 41.3 us
    pallas_call x1, Pallas kernels: 41.3 us -> 40.3 us  [per_device(): pl.pallas_call(functools.partial(kernel, step_factor), out_shape=(jax.Sha...]
where the time goes in v4:
time: 42.1 us; the launch traced here: 42 us
  Pallas kernels  41.3 us (98%)
  between operations  0.64 us (2%)
    pallas_call x1, Pallas kernels, per_device(): pl.pallas_call(functools.partial(kernel, step_factor), out_shape=(jax.Sha...  40.3 us
    pallas_call x1, Pallas kernels, per_device(): pl.pallas_call(write_out, out_shape=(jax.ShapeDtypeStruct((32, 128, NOCC)...  0.99 us

profile of v4, /device:TPU:160, one launch (start us, length us, event | category | flops | bytes accessed | tf_op | source)
XLA Modules:
  0.0 42.0 jit_solution(14328461573649928371)
XLA Ops:
  0.6 40.3 %shard_map.68 = (bf16[32,128,128]{2,1,0:T(8,128)(2,1)S(1)}, f32[1,32]{1,0:T(1,128)S(1)}) custom-call(bf16[256,2,64,128]{3,2,1,0:T(8,128)(2,1)} %v_hbm.1, s32[2,2,256]{2,1,0:T(2,128)} %bitcast.4, bf16[32,128,256]{2,1,0:T(8,128)(2,1)} %g_hbm.1, bf16[32,128,128]{2,1,0:T(8,128)(2,1)} %w_hbm.1, f32[32,256]{1,0:T(8,128)} %bitcast.3), custom_call_target="tpu_custom_call" | custom-call | tf_op jit(solution)/shard_map/pallas_call | solution.py:319
  41.0 1.0 %shard_map.69 = (bf16[32,128,128]{2,1,0:T(8,128)(2,1)}, f32[1,32]{1,0:T(1,128)}) custom-call(bf16[32,128,128]{2,1,0:T(8,128)(2,1)S(1)} %get-tuple-element.6.w_ref, f32[1,32]{1,0:T(1,128)S(1)} %get-tuple-element.7.e_ref), custom_call_target="tpu_custom_call" | custom-call | tf_op jit(solution)/shard_map/pallas_call | solution.py:356

commit v5 on v4

--- a/solution.py
+++ b/solution.py
@@ -151,7 +151,7 @@
     lo32 = lax.broadcasted_iota(jnp.int32, (32, 128), 1) < BLOCK
     o1 = {(h, d, r): slots() for h in range(2) for d in range(4) for r in range(2)}
     f1 = {(h, d, r): slots() for h in range(2) for d in (1, 2, 3) for r in range(2)}
-    fl = slots()
+    fl = [slots(), slots()]
 
     def rows_of(r, q):
         return pl.ds(r * HALF + q * 32, 32)
@@ -165,7 +165,7 @@
         for h in range(2):
             src = pp.at[walker(h, WAY[s], d), rows_of(r, q)]
             if d == 0:
-                send(src, last.at[core * 5 + s, rows_of(r, q)], dev(chip_of(h, WAY[s], 0), h), fl)
+                send(src, last.at[core * 5 + s, rows_of(r, q)], dev(chip_of(h, WAY[s], 0), h), fl[r])
             else:
                 send(src, fin1.at[h, d, r, s, q], dev(chip_of(h, WAY[s], 0), core), f1[h, d, r])
 
@@ -206,7 +206,8 @@
                 send_opp(d, r, q)
         for d in (2, 1) if r else (2, 1, 3, 0):
             send_own(d, r)
-    send(pp.at[2 * chip + other], last.at[10], dev(chip, other), fl)
+        rows = pl.ds(r * HALF, HALF)
+        send(pp.at[2 * chip + other, rows], last.at[10, rows], dev(chip, other), fl[r])
 
     arrive(ebuf.at[0, pl.ds(1, 3)], ex)
     ebuf[0, 0] = esend[0]
@@ -221,7 +222,7 @@
             arrive(fin1.at[h, d, r], f1[h, d, r])
             both = fin1[h, d, r, 0].astype(F32) + fin1[h, d, r, 1].astype(F32)
             s1[h, d, r] = (pp[walker(h, 0, d), rows].astype(F32) + both.reshape(HALF, 256)).astype(BF16)
-            send(s1.at[h, d, r], last.at[core * 5 + 1 + d, rows], dev(chip_of(h, 0, d), h), fl)
+            send(s1.at[h, d, r], last.at[core * 5 + 1 + d, rows], dev(chip_of(h, 0, d), h), fl[r])
 
     for d in (2, 1, 3):
         add_opp(d, 0)
@@ -244,16 +245,19 @@
     e_ref[...] = row[0:1, 0:32]
 
     mine = 2 * chip + core
-    arrive(last, fl)
-    for o in range(2):
-        own = jnp.where(core == o, pp[mine].astype(F32), last[10].astype(F32))
-        for n in range(5):
-            own = own + last[o * 5 + n].astype(F32)
-        full = step_factor * own
-        near, far = full[:, :128], full[:, 128:]
-        near = jnp.concatenate([near[:BLOCK], pltpu.roll(near[BLOCK:], BLOCK, 1)], axis=0)
-        pair = [near, far] if o == 0 else [far, near]
-        pot[o * 128:(o + 1) * 128, :] = jnp.concatenate(pair, axis=1).astype(BF16)
+    for r in range(2):
+        rows = pl.ds(r * HALF, HALF)
+        arrive(last.at[:, rows], fl[r])
+        for o in range(2):
+            own = jnp.where(core == o, pp[mine, rows].astype(F32), last[10, rows].astype(F32))
+            for n in range(5):
+                own = own + last[o * 5 + n, rows].astype(F32)
+            full = step_factor * own
+            near, far = full[:, :128], full[:, 128:]
+            if r == 1:
+                near = pltpu.roll(near, BLOCK, 1)
+            pair = [near, far] if o == 0 else [far, near]
+            pot[pl.ds(o * 128 + r * HALF, HALF), :] = jnp.concatenate(pair, axis=1).astype(BF16)
     arrive(tbuf.at[other], wi)
     start = tbuf[...].reshape(NORB, NOCC)
     term = start
@@ -297,7 +301,7 @@
     return (rows[0] + rows[1]) + (rows[2] + rows[3])
 
 
-SEMS = 40
+SEMS = 41
 
 
 def write_out(w_ref, e_ref, w_out, e_out, sem):

time: 42.1 us -> 42.1 us (level)
  no operation moved by 1% of the time
where the time goes in v5:
time: 42.1 us; the launch traced here: 42 us
  Pallas kernels  41.3 us (98%)
  between operations  0.64 us (2%)
    pallas_call x1, Pallas kernels, per_device(): pl.pallas_call(functools.partial(kernel, step_factor), out_shape=(jax.Sha...  40.3 us
    pallas_call x1, Pallas kernels, per_device(): pl.pallas_call(write_out, out_shape=(jax.ShapeDtypeStruct((32, 128, NOCC)...  0.99 us

profile of v5, /device:TPU:160, one launch (start us, length us, event | category | flops | bytes accessed | tf_op | source)
XLA Modules:
  0.0 42.0 jit_solution(2777725300279682529)
XLA Ops:
  0.6 40.3 %shard_map.68 = (bf16[32,128,128]{2,1,0:T(8,128)(2,1)S(1)}, f32[1,32]{1,0:T(1,128)S(1)}) custom-call(bf16[256,2,64,128]{3,2,1,0:T(8,128)(2,1)} %v_hbm.1, s32[2,2,256]{2,1,0:T(2,128)} %bitcast.4, bf16[32,128,256]{2,1,0:T(8,128)(2,1)} %g_hbm.1, bf16[32,128,128]{2,1,0:T(8,128)(2,1)} %w_hbm.1, f32[32,256]{1,0:T(8,128)} %bitcast.3), custom_call_target="tpu_custom_call" | custom-call | tf_op jit(solution)/shard_map/pallas_call | solution.py:323
  41.0 1.0 %shard_map.69 = (bf16[32,128,128]{2,1,0:T(8,128)(2,1)}, f32[1,32]{1,0:T(1,128)}) custom-call(bf16[32,128,128]{2,1,0:T(8,128)(2,1)S(1)} %get-tuple-element.6.w_ref, f32[1,32]{1,0:T(1,128)S(1)} %get-tuple-element.7.e_ref), custom_call_target="tpu_custom_call" | custom-call | tf_op jit(solution)/shard_map/pallas_call | solution.py:360

commit v6 on v5

--- a/solution.py
+++ b/solution.py
@@ -245,6 +245,9 @@
     e_ref[...] = row[0:1, 0:32]
 
     mine = 2 * chip + core
+    arrive(tbuf.at[other], wi)
+    start = tbuf[...].reshape(NORB, NOCC)
+    first_rows = {}
     for r in range(2):
         rows = pl.ds(r * HALF, HALF)
         arrive(last.at[:, rows], fl[r])
@@ -257,13 +260,16 @@
             if r == 1:
                 near = pltpu.roll(near, BLOCK, 1)
             pair = [near, far] if o == 0 else [far, near]
-            pot[pl.ds(o * 128 + r * HALF, HALF), :] = jnp.concatenate(pair, axis=1).astype(BF16)
-    arrive(tbuf.at[other], wi)
-    start = tbuf[...].reshape(NORB, NOCC)
+            piece = jnp.concatenate(pair, axis=1).astype(BF16)
+            pot[pl.ds(o * 128 + r * HALF, HALF), :] = piece
+            first_rows[o, r] = jnp.dot(piece, start, preferred_element_type=F32)
     term = start
     total = jnp.zeros((NORB, NOCC), F32)
     for degree in range(1, TAYLOR + 1):
-        product = jnp.dot(pot[...], term, preferred_element_type=F32)
+        if degree == 1:
+            product = jnp.concatenate([first_rows[o, r] for o in range(2) for r in range(2)], axis=0)
+        else:
+            product = jnp.dot(pot[...], term, preferred_element_type=F32)
         term = (product / degree).astype(BF16)
         total = total + term.astype(F32)
     nw[...] = (start.astype(F32) + total).astype(BF16).reshape(2, 128, NOCC)

time: 42.1 us -> 41.9 us (level)
  no operation moved by 1% of the time
where the time goes in v6:
time: 41.9 us
  Pallas kernels  41.2 us (98%)
  between operations  0.64 us (2%)
    pallas_call x1, Pallas kernels, per_device(): pl.pallas_call(functools.partial(kernel, step_factor), out_shape=(jax.Sha...  40.2 us
    pallas_call x1, Pallas kernels, per_device(): pl.pallas_call(write_out, out_shape=(jax.ShapeDtypeStruct((32, 128, NOCC)...  0.99 us

profile of v6, /device:TPU:160, one launch (start us, length us, event | category | flops | bytes accessed | tf_op | source)
XLA Modules:
  0.0 41.9 jit_solution(651789135130729555)
XLA Ops:
  0.6 40.2 %shard_map.68 = (bf16[32,128,128]{2,1,0:T(8,128)(2,1)S(1)}, f32[1,32]{1,0:T(1,128)S(1)}) custom-call(bf16[256,2,64,128]{3,2,1,0:T(8,128)(2,1)} %v_hbm.1, s32[2,2,256]{2,1,0:T(2,128)} %bitcast.4, bf16[32,128,256]{2,1,0:T(8,128)(2,1)} %g_hbm.1, bf16[32,128,128]{2,1,0:T(8,128)(2,1)} %w_hbm.1, f32[32,256]{1,0:T(8,128)} %bitcast.3), custom_call_target="tpu_custom_call" | custom-call | tf_op jit(solution)/shard_map/pallas_call | solution.py:329
  40.9 1.0 %shard_map.69 = (bf16[32,128,128]{2,1,0:T(8,128)(2,1)}, f32[1,32]{1,0:T(1,128)}) custom-call(bf16[32,128,128]{2,1,0:T(8,128)(2,1)S(1)} %get-tuple-element.6.w_ref, f32[1,32]{1,0:T(1,128)S(1)} %get-tuple-element.7.e_ref), custom_call_target="tpu_custom_call" | custom-call | tf_op jit(solution)/shard_map/pallas_call | solution.py:366
